TPU v7x, 128 devices: a whole 4x4x4 slice. The times are simulated.
128 devices in a mesh: seq: 64 (over z, y, x), exp: 2 (over core).
Axes of the slice: x: 4, y: 4, z: 4, core: 2. Of those that a mesh axis runs over, the one named last changes fastest.
Arguments:
- queries: bfloat16 [16384, 1024], P('seq', 'exp'), may hold values from -170 to 170
- keys: bfloat16 [16384, 1024], P('seq', 'exp'), may hold values from -5 to 5
- values: bfloat16 [16384, 1024], P('seq', 'exp'), may hold values from -6 to 6
- resid: bfloat16 [16384, 2048], P(('seq', 'exp')), may hold values from -6 to 6
- pair_ids: int32 [16384], replicated, may hold values from 0 to 63, never falling along the last dimension, each value on 1 to 512 neighbouring positions
- out_weight: bfloat16 [1024, 2048], P('exp'), may hold values from -0.1875 to 0.1875
- norm_gain: float32 [2048], replicated, may hold values from 0.5 to 1.5
- experts: int32 [16384, 6], P(('seq', 'exp')), may hold values from 0 to 63, all different within a row; in each aligned block of 128 rows (0 to 127, 128 to 255, ...) at most 24 rows name the same one
- gates: float32 [16384, 6], P(('seq', 'exp')), may hold values from 0.05 to 0.5
- w_gate: bfloat16 [64, 2048, 704], P('seq', None, 'exp'), may hold values from -0.125 to 0.125
- w_up: bfloat16 [64, 2048, 704], P('seq', None, 'exp'), may hold values from -0.125 to 0.125
- w_down: bfloat16 [64, 704, 2048], P('seq', 'exp'), may hold values from -0.21875 to 0.21875
Outputs:
- mixed: bfloat16 [16384, 2048], P(('seq', 'exp'))
Inputs may be any that keep to these rules, and one draw needn't show every extreme that they name: In the aligned blocks of 128 rows no expert is named more than 24 times, a bound that some block reaches; each row names 6 different experts. `pair_ids`: pair numbers never fall along the sequence; each pair has 1 to 512 tokens, one exactly that many.
All inputs are finite; a program needn't handle non-finite values.
Results may differ from a plain program's by a relative error of at most 0.012.
Values may be sent and summed in bfloat16 or wider, within the bound.
A program may use at most 128 MiB of HBM per device.

v0:
```python
import math
import jax
import jax.numpy as jnp
from jax import lax
from jax.sharding import PartitionSpec as P

HD = 128
TOP = 6


def with_halo(cells, sides, width):
    for axis, dim in sides:
        count = lax.axis_size(axis)
        ends = count - 1
        head = lax.slice_in_dim(cells, 0, width, axis=dim)
        tail = lax.slice_in_dim(cells, cells.shape[dim] - width, cells.shape[dim], axis=dim)
        cells = jnp.concatenate(
            [
                lax.ppermute(tail, axis, [(i, (i + 1) % count) for i in range(ends)]),
                cells,
                lax.ppermute(head, axis, [((i + 1) % count, i) for i in range(ends)]),
            ],
            axis=dim,
        )
    return cells


def send_back(result):
    return lax.all_to_all(result, "seq", split_axis=0, concat_axis=0, tiled=True)


def shards(
    queries,
    keys,
    values,
    resid,
    pair_ids,
    out_weight,
    norm_gain,
    experts,
    gates,
    w_gate,
    w_up,
    w_down,
):
    tok_rows = queries.shape[0]
    local_width = queries.shape[1]
    local_heads = local_width // HD
    shard = lax.axis_index("seq")
    stacked = jnp.stack([keys, values])
    widened = with_halo(stacked, (("seq", 1),), tok_rows)
    id_pad = jnp.pad(pair_ids, (tok_rows, tok_rows), constant_values=-1)
    key_ids = lax.dynamic_slice_in_dim(id_pad, shard * tok_rows, 3 * tok_rows, 0)
    query_ids = lax.dynamic_slice_in_dim(id_pad, shard * tok_rows + tok_rows, tok_rows, 0)
    query_pos = jnp.arange(tok_rows, dtype=jnp.int32) + tok_rows
    key_pos = jnp.arange(3 * tok_rows, dtype=jnp.int32)
    allowed = (query_ids[:, None] == key_ids[None, :]) & (
        jnp.abs(query_pos[:, None] - key_pos[None, :]) < tok_rows
    )
    query_heads = queries.reshape(tok_rows, local_heads, HD)
    key_heads = widened[0].reshape(3 * tok_rows, local_heads, HD)
    value_heads = widened[1].reshape(3 * tok_rows, local_heads, HD)
    score = jnp.einsum(
        "qhd,khd->hqk", query_heads, key_heads, preferred_element_type=jnp.float32
    ) / math.sqrt(HD)
    score = jnp.where(allowed[None], score, -jnp.inf)
    top = jnp.max(score, axis=-1, keepdims=True)
    weights = jnp.exp(score - top)
    probs = (weights / jnp.sum(weights, axis=-1, keepdims=True)).astype(jnp.bfloat16)
    attended = jnp.einsum("hqk,khd->qhd", probs, value_heads, preferred_element_type=jnp.float32)
    attended = attended.reshape(tok_rows, local_width).astype(jnp.bfloat16)
    moe_rows = resid.shape[0]
    projected = lax.psum(
        jnp.dot(attended, out_weight, preferred_element_type=jnp.float32).astype(jnp.bfloat16),
        "exp",
    ).astype(jnp.float32)
    projected = lax.dynamic_slice_in_dim(projected, lax.axis_index("exp") * moe_rows, moe_rows, 0)
    stream = resid.astype(jnp.float32) + projected
    meansq = jnp.mean(stream * stream, axis=-1, keepdims=True)
    normed = (stream * lax.rsqrt(meansq + 1e-05) * norm_gain).astype(jnp.bfloat16)
    n_experts = lax.axis_size("seq") * w_gate.shape[0]
    capacity = 2 * moe_rows * TOP // n_experts
    flat_experts = experts.reshape(-1)
    onehot = (flat_experts[:, None] == jnp.arange(n_experts, dtype=jnp.int32)[None, :]).astype(
        jnp.int32
    )
    ranks = jnp.cumsum(onehot, axis=0) - onehot
    slot_index = jnp.sum(ranks * onehot, axis=1)
    destination = flat_experts * capacity + slot_index
    token_of = jnp.arange(moe_rows * TOP, dtype=jnp.int32) // TOP
    outgoing = (
        jnp.zeros((n_experts * capacity, normed.shape[1]), jnp.bfloat16)
        .at[destination]
        .set(normed[token_of])
    )
    outgoing = outgoing.reshape(n_experts, capacity, normed.shape[1])
    arrived = lax.all_to_all(outgoing, "seq", split_axis=0, concat_axis=0, tiled=True)
    sources = arrived.shape[0]
    slots = arrived.shape[1]
    inputs = arrived.reshape(sources * slots, arrived.shape[2])
    group = lax.all_gather(inputs, "exp", axis=0, tiled=True)
    gate_part = jnp.dot(group, w_gate[0], preferred_element_type=jnp.float32)
    up_part = jnp.dot(group, w_up[0], preferred_element_type=jnp.float32)
    act = (jax.nn.silu(gate_part) * up_part).astype(jnp.bfloat16)
    result = lax.psum_scatter(
        jnp.dot(act, w_down[0], preferred_element_type=jnp.float32).astype(jnp.bfloat16),
        "exp",
        scatter_dimension=0,
        tiled=True,
    )
    result = result.reshape(sources, slots, result.shape[1])
    back = send_back(result)
    gathered = back.reshape(n_experts * capacity, back.shape[2])[destination]
    gathered = gathered.reshape(moe_rows, TOP, gathered.shape[1]).astype(jnp.float32)
    mixture = jnp.einsum("mk,mkd->md", gates, gathered)
    return (stream + mixture).astype(jnp.bfloat16)


def solution(mesh):
    in_specs = (
        P("seq", "exp"),
        P("seq", "exp"),
        P("seq", "exp"),
        P(("seq", "exp"), None),
        P(),
        P("exp", None),
        P(),
        P(("seq", "exp"), None),
        P(("seq", "exp"), None),
        P("seq", None, "exp"),
        P("seq", None, "exp"),
        P("seq", "exp", None),
    )
    out_specs = P(("seq", "exp"), None)
    return jax.shard_map(shards, mesh=mesh, in_specs=in_specs, out_specs=out_specs, check_vma=False)
```

profile of v0, /device:TPU:10, one launch (start us, length us, event | category | flops | bytes accessed | tf_op | source)
XLA Modules:
  0.0 383.7 jit_solution(15358219397726013312)
XLA Ops:
  6.5 1.2 copy.16
  7.8 1.1 copy.17
  8.9 0.1 pad_maximum_fusion.1
  8.9 3.4 collective-permute-start
  12.3 2.4 collective-permute-start.1
  14.8 0.8 pad_dynamic-slice_fusion.1
  15.6 0.8 pad_dynamic-slice_fusion
  16.4 0.3 fusion.18
  16.6 0.0 copy-start.4
  16.6 7.9 %collective-permute-done = bf16[2,256,512]{1,2,0:T(8,128)(2,1)} collective-permute-done((bf16[2,256,512]{1,2,0:T(8,128)(2,1)S(1)}, bf16[2,256,512]{1,2,0:T(8,128)(2,1)}, u32[]{:S(2)}, u32[]{:S(2)}) %collective-permute-start) | collective-permute-done | bytes 524320 | tf_op jit(solution)/shard_map/ppermute | solution.py:19
  24.6 3.1 collective-permute-done.1
  27.7 1.3 pad_maximum_fusion
  29.0 0.1 fusion.31
  29.1 0.6 fusion.19
  29.8 1.6 fusion.32
  31.4 0.4 fusion.16
  31.8 0.0 copy-start.2
  31.8 0.0 copy-start.6
  31.8 1.7 convolution_convert_fusion.1
  33.6 0.0 all-reduce.3.cloned.1.call-update
  33.6 0.0 all-gather.2.cloned.1.call-start
  33.6 0.1 copy.22
  33.8 0.1 eq.49
  33.9 0.1 eq.45
  34.1 1.8 reduce-window.6
  35.9 0.3 slice_reduce_fusion
  36.2 0.1 copy.21
  36.3 0.1 mul.56
  36.5 0.1 fusion.24
  36.6 28.0 %all-reduce.3.cloned.1.call-done = bf16[256,2048]{1,0:T(8,128)(2,1)} async-done(((bf16[256,2048]{1,0:T(8,128)(2,1)}), bf16[256,2048]{1,0:T(8,128)(2,1)}) %all-reduce.3.cloned.1.call-update) | async-done | bytes 1048592 | tf_op jit(solution)/shard_map/psum | solution.py:73
  64.6 1.3 multiply_reduce_fusion
  65.9 1.3 multiply_convert_fusion
  67.2 24.2 %scatter_custom_fusion = bf16[1536,2048]{1,0:T(8,128)(2,1)} fusion(s32[768]{0:T(1024)S(1)} %fusion.26, bf16[128,2048]{1,0:T(8,128)(2,1)S(1)} %multiply_convert_fusion, s32[1024]{0:T(1024)S(1)} %pad_clamp_fusion.1, bf16[]{:T(256)} %constant.50.clone.1), kind=kCustom, calls=%fused_computation.8 | custom fusion | bytes 6291458 | tf_op jit(solution)/shard_map/scatter | solution.py:94
  91.4 84.0 %all_to_all.10 = bf16[64,24,2048]{2,1,0:T(8,128)(2,1)} all-to-all(bf16[64,24,2048]{2,1,0:T(8,128)(2,1)} %bitcast.73), channel_id=1, replica_groups=mesh['seq'=64,'exp'=2] {'seq'}, dimensions={0} | all-to-all | bytes 12582912 | tf_op jit(solution)/shard_map/all_to_all | solution.py:97
  175.3 0.0 all-gather.2.cloned.1.call-update
  175.4 0.0 reduce-scatter.2.cloned.1.call-start
  175.4 26.4 %all-gather.2.cloned.1.call-done = bf16[3072,2048]{1,0:T(8,128)(2,1)} async-done(((bf16[1536,2048]{1,0:T(8,128)(2,1)}), bf16[3072,2048]{1,0:T(8,128)(2,1)}) %all-gather.2.cloned.1.call-update) | async-done | bytes 12582928 | tf_op jit(solution)/shard_map/all_gather | solution.py:101
  201.8 9.8 %fusion.14 = f32[3072,352]{0,1:T(8,128)} fusion(bf16[3072,2048]{1,0:T(8,128)(2,1)} %all-gather.2.cloned.1.call-done, bf16[1,2048,352]{1,2,0:T(8,128)(2,1)S(1)} %copy-done.8), kind=kOutput, calls=%fused_computation.23 | convolution fusion | flops 4429185024 | bytes 18350080 | tf_op jit(solution)/shard_map/dot_general | solution.py:102
  211.6 18.6 %convolution_convert_fusion = bf16[3072,2048]{1,0:T(8,128)(2,1)} fusion(bf16[3072,2048]{1,0:T(8,128)(2,1)} %all-gather.2.cloned.1.call-done, f32[3072,352]{0,1:T(8,128)} %fusion.14, bf16[1,352,2048]{2,1,0:T(8,128)(2,1)} %param.23, bf16[1,2048,352]{1,2,0:T(8,128)(2,1)} %param.22), kind=kOutput, calls=%fused_computation.4 | convolution fusion | flops 8871149568 | bytes 32374784 | tf_op jit(solution)/shard_map/dot_general | solution.py:106
  230.2 0.0 reduce-scatter.2.cloned.1.call-update
  230.2 25.7 %reduce-scatter.2.cloned.1.call-done = bf16[1536,2048]{1,0:T(8,128)(2,1)} async-done(((bf16[3072,2048]{1,0:T(8,128)(2,1)}), bf16[1536,2048]{1,0:T(8,128)(2,1)}) %reduce-scatter.2.cloned.1.call-update) | async-done | bytes 6291472 | tf_op jit(solution)/shard_map/reduce_scatter | solution.py:105
  255.9 10.7 %all-to-all-start.1 = ((bf16[64,24,2048]{2,1,0:T(8,128)(2,1)}), bf16[64,24,2048]{2,1,0:T(8,128)(2,1)}, u32[]{:S(2)}, u32[]{:S(2)}) async-start(bf16[64,24,2048]{2,1,0:T(8,128)(2,1)} %bitcast.74), calls=%async_computation.2 | async-start | bytes 12582912 | tf_op jit(solution)/shard_map/all_to_all | solution.py:29
  266.6 0.2 copy.27
  266.8 88.4 %all-to-all-done.1 = bf16[64,24,2048]{2,1,0:T(8,128)(2,1)} async-done(((bf16[64,24,2048]{2,1,0:T(8,128)(2,1)}), bf16[64,24,2048]{2,1,0:T(8,128)(2,1)}, u32[]{:S(2)}, u32[]{:S(2)}) %all-to-all-start.1) | async-done | bytes 6291488 | tf_op jit(solution)/shard_map/all_to_all | solution.py:29
  355.2 10.8 %gather_fusion = bf16[768,2048]{1,0:T(8,128)(2,1)} fusion(bf16[1536,2048]{1,0:T(8,128)(2,1)} %bitcast.14, s32[1024]{0:T(1024)S(1)} %pad_clamp_fusion), kind=kCustom, calls=%fused_computation.1 | custom fusion | bytes 6294528 | tf_op jit(solution)/shard_map/gather | solution.py:113
  365.9 6.4 %reshape.179 = bf16[128,6,2048]{2,1,0:T(8,128)(2,1)} reshape(bf16[768,2048]{1,0:T(8,128)(2,1)} %gather_fusion) | data formatting | bytes 6291456 | tf_op jit(solution)/shard_map/reshape | solution.py:114
  372.4 3.5 fusion.33
  375.9 1.3 fusion.17
  (24 shorter events, 0.1 us)
Async XLA Ops:
  6.5 25.3 %copy-start = (bf16[512,2048]{1,0:T(8,128)(2,1)S(1)}, bf16[512,2048]{1,0:T(8,128)(2,1)}, u32[]{:S(2)}) copy-start(bf16[512,2048]{1,0:T(8,128)(2,1)} %param.17) | copy-start | bytes 6291460
  6.5 58.0 %all-reduce.3.cloned.1.call-start = ((), (), s32[]{:S(2)}) async-start(), calls=%async_computation.3 | async-start | bytes 2097152 | tf_op jit(solution)/shard_map/psum | solution.py:73
  8.9 15.7 %collective-permute-start = (bf16[2,256,512]{1,2,0:T(8,128)(2,1)S(1)}, bf16[2,256,512]{1,2,0:T(8,128)(2,1)}, u32[]{:S(2)}, u32[]{:S(2)}) collective-permute-start(bf16[2,256,512]{1,2,0:T(8,128)(2,1)S(1)} %pad_maximum_fusion.1), channel_id=1, source_target_pairs={{0,2},{2,4},{4,6},{6,8},{8,10},{10,12},{12,14},{14,16},{16,18},{18... | collective-permute-start | bytes 1572872 | tf_op jit(solution)/shard_map/ppermute | solution.py:19
  12.3 15.4 %collective-permute-start.1 = (bf16[2,256,512]{1,2,0:T(8,128)(2,1)S(1)}, bf16[2,256,512]{1,2,0:T(8,128)(2,1)}, u32[]{:S(2)}, u32[]{:S(2)}) collective-permute-start(bf16[2,256,512]{1,2,0:T(8,128)(2,1)S(1)} %pad_maximum_fusion.1), channel_id=1, source_target_pairs={{2,0},{4,2},{6,4},{8,6},{10,8},{12,10},{14,12},{16,14},{18,16},{20... | collective-permute-start | bytes 1572872 | tf_op jit(solution)/shard_map/ppermute | solution.py:21
  16.6 12.5 %copy-start.4 = (bf16[256,512]{1,0:T(8,128)(2,1)S(1)}, bf16[256,512]{1,0:T(8,128)(2,1)}, u32[]{:S(2)}) copy-start(bf16[256,512]{1,0:T(8,128)(2,1)} %param.12) | copy-start | bytes 786436
  31.8 1.9 copy-start.5
  31.8 32.8 %copy-start.2 = (bf16[128,2048]{1,0:T(8,128)(2,1)S(1)}, bf16[128,2048]{1,0:T(8,128)(2,1)}, u32[]{:S(2)}) copy-start(bf16[128,2048]{1,0:T(8,128)(2,1)} %param.15) | copy-start | bytes 1572868
  31.8 34.1 %copy-start.6 = (f32[2048]{0:T(1024)S(1)}, f32[2048]{0:T(1024)}, u32[]{:S(2)}) copy-start(f32[2048]{0:T(1024)} %param.18) | copy-start | bytes 24580
  33.6 168.2 %all-gather.2.cloned.1.call-start = ((), (), s32[]{:S(2)}) async-start(), calls=%async_computation.4 | async-start | bytes 18874368 | tf_op jit(solution)/shard_map/all_gather | solution.py:101
  175.3 26.5 %copy-start.8 = (bf16[1,2048,352]{1,2,0:T(8,128)(2,1)S(1)}, bf16[1,2048,352]{1,2,0:T(8,128)(2,1)}, u32[]{:S(2)}) copy-start(bf16[1,2048,352]{1,2,0:T(8,128)(2,1)} %param.21) | copy-start | bytes 4325380
  175.4 80.5 %reduce-scatter.2.cloned.1.call-start = ((), (), s32[]{:S(2)}) async-start(), calls=%async_computation.5 | async-start | bytes 18874368 | tf_op jit(solution)/shard_map/reduce_scatter | solution.py:105
  255.9 10.7 %copy-start.7 = (f32[128,6]{0,1:T(8,128)S(1)}, f32[128,6]{0,1:T(8,128)}, u32[]{:S(2)}) copy-start(f32[128,6]{0,1:T(8,128)} %param.20) | copy-start | bytes 9220
  255.9 99.3 %all-to-all-start.1 = ((bf16[64,24,2048]{2,1,0:T(8,128)(2,1)}), bf16[64,24,2048]{2,1,0:T(8,128)(2,1)}, u32[]{:S(2)}, u32[]{:S(2)}) async-start(bf16[64,24,2048]{2,1,0:T(8,128)(2,1)} %bitcast.74), calls=%async_computation.2 | async-start | bytes 12582912 | tf_op jit(solution)/shard_map/all_to_all | solution.py:29
  365.9 11.2 %copy-start.1 = (bf16[512,2048]{1,0:T(8,128)(2,1)S(1)}, bf16[512,2048]{1,0:T(8,128)(2,1)}, u32[]{:S(2)}) copy-start(bf16[512,2048]{1,0:T(8,128)(2,1)} %param.17) | copy-start | bytes 6291460
  372.4 3.5 copy-start.3
Sparse Core Ops, SparseCore 0:
  33.7 30.8 all-reduce.2
  175.5 26.2 all-gather.1
  230.3 25.5 reduce-scatter.1
where the time goes:
time: 384 us
  waiting for transfers between devices  180 us (47%)
  blocking collectives  84 us (22%)
  local copies, waits for them, and re-layouts  45.7 us (12%)
  matrix products  34.6 us (9%)
  starting transfers between devices  16.6 us (4%)
  between operations  13.4 us (3%)
  other arithmetic  9.89 us (3%)
    all_to_all x1, waiting for transfers between devices, send_back(): lax.all_to_all(result, 'seq', split_axis=0, concat_axis=0, tiled=True)  88.4 us
    all_to_all x1, blocking collectives, shards(): lax.all_to_all(outgoing, 'seq', split_axis=0, concat_axis=0, tiled=True)  84 us
    psum x1, waiting for transfers between devices, shards(): lax.psum(jnp.dot(attended, out_weight, preferred_element_type=jnp.float32...  28 us
    all_gather x1, waiting for transfers between devices, shards(): group = lax.all_gather(inputs, 'exp', axis=0, tiled=True)  26.4 us
    reduce_scatter x1, waiting for transfers between devices, shards(): lax.psum_scatter(jnp.dot(act, w_down[0], preferred_element_type=jnp.float...  25.7 us
    scatter x1, local copies, waits for them, and re-layouts, shards(): outgoing = jnp.zeros((n_experts * capacity, normed.shape[1]), jnp.bfloat1...  24.2 us
    dot_general x1, matrix products, shards(): jnp.dot(act, w_down[0], preferred_element_type=jnp.float32)  18.6 us
    gather x1, local copies, waits for them, and re-layouts, shards(): gathered = back.reshape(n_experts * capacity, back.shape[2])[destination]  10.8 us
  transfers between devices with their start and end apart: 6, of which 6 were waited for; matrix products, arithmetic and copies ran while one was open for 1% of the time, Pallas kernels for 0%

commit v1 on v0

--- a/solution.py
+++ b/solution.py
@@ -98,7 +98,9 @@
     sources = arrived.shape[0]
     slots = arrived.shape[1]
     inputs = arrived.reshape(sources * slots, arrived.shape[2])
-    group = lax.all_gather(inputs, "exp", axis=0, tiled=True)
+    group = jnp.concatenate(
+        lax.all_to_all(jnp.stack([inputs] * lax.axis_size("exp")), "exp", 0, 0), axis=0
+    )
     gate_part = jnp.dot(group, w_gate[0], preferred_element_type=jnp.float32)
     up_part = jnp.dot(group, w_up[0], preferred_element_type=jnp.float32)
     act = (jax.nn.silu(gate_part) * up_part).astype(jnp.bfloat16)

time: 384 us -> 371 us (0.966)
  waiting for transfers between devices: 180 us -> 149 us
  blocking collectives: 84 us -> 97.8 us
  local copies, waits for them, and re-layouts: 45.7 us -> 50.2 us
    all_gather x1 -> x0, waiting for transfers between devices: 26.4 us -> none  [shards(): group = lax.all_gather(inputs, 'exp', axis=0, tiled=True)]
    all_to_all x0 -> x1, blocking collectives: none -> 14 us  [shards(): lax.all_to_all(jnp.stack([inputs] * lax.axis_size('exp')), 'exp', 0, 0)]
    unnamed x22 -> x24, local copies, waits for them, and re-layouts: 2.62 us -> 7.1 us
  transfers between devices with their start and end apart: 6 -> 5, of which waited for: 6 -> 5; matrix products, arithmetic and copies ran while one was open for 1% -> 1% of each run, Pallas kernels for 0% -> 0%
where the time goes in v1:
time: 371 us; the launch traced here: 369 us
  waiting for transfers between devices  149 us (40%)
  blocking collectives  97.8 us (26%)
  local copies, waits for them, and re-layouts  50.2 us (14%)
  matrix products  31.2 us (8%)
  starting transfers between devices  16.6 us (4%)
  between operations  13.7 us (4%)
  other arithmetic  11 us (3%)
    all_to_all x1, waiting for transfers between devices, send_back(): lax.all_to_all(result, 'seq', split_axis=0, concat_axis=0, tiled=True)  86.8 us
    all_to_all x1, blocking collectives, shards(): lax.all_to_all(outgoing, 'seq', split_axis=0, concat_axis=0, tiled=True)  83.9 us
    psum x1, waiting for transfers between devices, shards(): lax.psum(jnp.dot(attended, out_weight, preferred_element_type=jnp.float32...  28 us
    scatter x1, local copies, waits for them, and re-layouts, shards(): outgoing = jnp.zeros((n_experts * capacity, normed.shape[1]), jnp.bfloat1...  24.2 us
    reduce_scatter x1, waiting for transfers between devices, shards(): lax.psum_scatter(jnp.dot(act, w_down[0], preferred_element_type=jnp.float...  23 us
    dot_general x1, matrix products, shards(): jnp.dot(act, w_down[0], preferred_element_type=jnp.float32)  18.6 us
    all_to_all x1, blocking collectives, shards(): lax.all_to_all(jnp.stack([inputs] * lax.axis_size('exp')), 'exp', 0, 0)  14 us
    gather x1, local copies, waits for them, and re-layouts, shards(): gathered = back.reshape(n_experts * capacity, back.shape[2])[destination]  10.8 us
  transfers between devices with their start and end apart: 5, of which 5 were waited for; matrix products, arithmetic and copies ran while one was open for 1% of the time, Pallas kernels for 0%

profile of v1, /device:TPU:10, one launch (start us, length us, event | category | flops | bytes accessed | tf_op | source)
XLA Modules:
  0.0 369.4 jit_solution(17330567266078570123)
XLA Ops:
  6.5 1.2 copy.16
  7.8 1.1 copy.17
  8.9 0.1 pad_maximum_fusion.2
  8.9 3.4 collective-permute-start
  12.3 2.4 collective-permute-start.1
  14.8 0.8 pad_dynamic-slice_fusion.1
  15.6 0.8 pad_dynamic-slice_fusion
  16.4 0.3 fusion.18
  16.6 0.0 copy-start.5
  16.6 7.9 %collective-permute-done = bf16[2,256,512]{1,2,0:T(8,128)(2,1)} collective-permute-done((bf16[2,256,512]{1,2,0:T(8,128)(2,1)S(1)}, bf16[2,256,512]{1,2,0:T(8,128)(2,1)}, u32[]{:S(2)}, u32[]{:S(2)}) %collective-permute-start) | collective-permute-done | bytes 524320 | tf_op jit(solution)/shard_map/ppermute | solution.py:19
  24.6 3.1 collective-permute-done.1
  27.7 1.3 pad_maximum_fusion.1
  29.0 0.1 fusion.31
  29.1 0.6 fusion.19
  29.8 1.6 fusion.32
  31.4 0.4 fusion.16
  31.8 0.0 copy-start.3
  31.8 0.0 copy-start.7
  31.8 1.7 convolution_convert_fusion.1
  33.6 0.0 all-reduce.3.cloned.1.call-update
  33.6 0.0 reduce-scatter.2.cloned.1.call-start
  33.6 0.1 copy.22
  33.8 0.1 eq.49
  33.9 0.1 eq.45
  34.1 1.8 reduce-window.6
  35.9 0.3 slice_reduce_fusion
  36.2 0.1 copy.21
  36.3 0.1 mul.56
  36.5 0.1 fusion.24
  36.6 28.0 %all-reduce.3.cloned.1.call-done = bf16[256,2048]{1,0:T(8,128)(2,1)} async-done(((bf16[256,2048]{1,0:T(8,128)(2,1)}), bf16[256,2048]{1,0:T(8,128)(2,1)}) %all-reduce.3.cloned.1.call-update) | async-done | bytes 1048592 | tf_op jit(solution)/shard_map/psum | solution.py:73
  64.6 1.3 multiply_reduce_fusion
  65.9 1.3 multiply_convert_fusion
  67.2 24.2 %scatter_custom_fusion = bf16[1536,2048]{1,0:T(8,128)(2,1)} fusion(s32[768]{0:T(1024)S(1)} %fusion.26, bf16[128,2048]{1,0:T(8,128)(2,1)S(1)} %multiply_convert_fusion, s32[1024]{0:T(1024)S(1)} %pad_clamp_fusion.1, bf16[]{:T(256)} %constant.50.clone.1), kind=kCustom, calls=%fused_computation.9 | custom fusion | bytes 6291458 | tf_op jit(solution)/shard_map/scatter | solution.py:94
  91.4 83.9 %all_to_all.15 = bf16[64,24,2048]{2,1,0:T(8,128)(2,1)S(1)} all-to-all(bf16[64,24,2048]{2,1,0:T(8,128)(2,1)} %bitcast.73), channel_id=1, replica_groups=mesh['seq'=64,'exp'=2] {'seq'}, dimensions={0} | all-to-all | bytes 12582912 | tf_op jit(solution)/shard_map/all_to_all | solution.py:97
  175.2 1.2 pad_maximum_fusion
  176.4 14.0 %all_to_all.16 = bf16[2,1536,2048]{2,1,0:T(8,128)(2,1)S(1)} all-to-all(bf16[2,1536,2048]{2,1,0:T(8,128)(2,1)S(1)} %pad_maximum_fusion), channel_id=1, replica_groups=mesh['seq'=64,'exp'=2] {'exp'}, dimensions={0} | all-to-all | bytes 25165824 | tf_op jit(solution)/shard_map/all_to_all | solution.py:102
  190.4 4.5 %copy-done.2 = bf16[2,1536,2048]{2,1,0:T(8,128)(2,1)} copy-done((bf16[2,1536,2048]{2,1,0:T(8,128)(2,1)}, bf16[2,1536,2048]{2,1,0:T(8,128)(2,1)S(1)}, u32[]{:S(2)}) %copy-start.2) | copy-done | bytes 12582936
  194.9 6.3 %fusion.14 = f32[3072,352]{0,1:T(8,128)} fusion(bf16[3072,2048]{1,0:T(8,128)(2,1)S(1)} %bitcast.75, bf16[1,2048,352]{1,2,0:T(8,128)(2,1)S(1)} %copy-done.9), kind=kOutput, calls=%fused_computation.24 | convolution fusion | flops 4429185024 | bytes 18350080 | tf_op jit(solution)/shard_map/dot_general | solution.py:104
  201.2 18.6 %convolution_convert_fusion = bf16[3072,2048]{1,0:T(8,128)(2,1)} fusion(bf16[3072,2048]{1,0:T(8,128)(2,1)} %bitcast.76, f32[3072,352]{0,1:T(8,128)} %fusion.14, bf16[1,352,2048]{2,1,0:T(8,128)(2,1)} %param.23, bf16[1,2048,352]{1,2,0:T(8,128)(2,1)} %param.22), kind=kOutput, calls=%fused_computation.5 | convolution fusion | flops 8871149568 | bytes 32374784 | tf_op jit(solution)/shard_map/dot_general | solution.py:108
  219.8 0.0 reduce-scatter.2.cloned.1.call-update
  219.8 23.0 %reduce-scatter.2.cloned.1.call-done = bf16[1536,2048]{1,0:T(8,128)(2,1)} async-done(((bf16[3072,2048]{1,0:T(8,128)(2,1)}), bf16[1536,2048]{1,0:T(8,128)(2,1)}) %reduce-scatter.2.cloned.1.call-update) | async-done | bytes 6291472 | tf_op jit(solution)/shard_map/reduce_scatter | solution.py:107
  242.8 10.7 %all-to-all-start.2 = ((bf16[64,24,2048]{2,1,0:T(8,128)(2,1)}), bf16[64,24,2048]{2,1,0:T(8,128)(2,1)}, u32[]{:S(2)}, u32[]{:S(2)}) async-start(bf16[64,24,2048]{2,1,0:T(8,128)(2,1)} %bitcast.77), calls=%async_computation.3 | async-start | bytes 12582912 | tf_op jit(solution)/shard_map/all_to_all | solution.py:29
  253.6 0.2 copy.27
  253.7 86.8 %all-to-all-done.2 = bf16[64,24,2048]{2,1,0:T(8,128)(2,1)} async-done(((bf16[64,24,2048]{2,1,0:T(8,128)(2,1)}), bf16[64,24,2048]{2,1,0:T(8,128)(2,1)}, u32[]{:S(2)}, u32[]{:S(2)}) %all-to-all-start.2) | async-done | bytes 6291488 | tf_op jit(solution)/shard_map/all_to_all | solution.py:29
  340.5 10.8 %gather_fusion = bf16[768,2048]{1,0:T(8,128)(2,1)} fusion(bf16[1536,2048]{1,0:T(8,128)(2,1)} %bitcast.15, s32[1024]{0:T(1024)S(1)} %pad_clamp_fusion), kind=kCustom, calls=%fused_computation.1 | custom fusion | bytes 6294528 | tf_op jit(solution)/shard_map/gather | solution.py:115
  351.3 6.4 %reshape.179 = bf16[128,6,2048]{2,1,0:T(8,128)(2,1)} reshape(bf16[768,2048]{1,0:T(8,128)(2,1)} %gather_fusion) | data formatting | bytes 6291456 | tf_op jit(solution)/shard_map/reshape | solution.py:116
  357.7 3.5 fusion.33
  361.3 1.3 fusion.17
  (25 shorter events, 0.2 us)
Async XLA Ops:
  6.5 25.3 %copy-start = (bf16[512,2048]{1,0:T(8,128)(2,1)S(1)}, bf16[512,2048]{1,0:T(8,128)(2,1)}, u32[]{:S(2)}) copy-start(bf16[512,2048]{1,0:T(8,128)(2,1)} %param.17) | copy-start | bytes 6291460
  6.5 58.0 %all-reduce.3.cloned.1.call-start = ((), (), s32[]{:S(2)}) async-start(), calls=%async_computation.4 | async-start | bytes 2097152 | tf_op jit(solution)/shard_map/psum | solution.py:73
  8.9 15.7 %collective-permute-start = (bf16[2,256,512]{1,2,0:T(8,128)(2,1)S(1)}, bf16[2,256,512]{1,2,0:T(8,128)(2,1)}, u32[]{:S(2)}, u32[]{:S(2)}) collective-permute-start(bf16[2,256,512]{1,2,0:T(8,128)(2,1)S(1)} %pad_maximum_fusion.2), channel_id=1, source_target_pairs={{0,2},{2,4},{4,6},{6,8},{8,10},{10,12},{12,14},{14,16},{16,18},{18... | collective-permute-start | bytes 1572872 | tf_op jit(solution)/shard_map/ppermute | solution.py:19
  12.3 15.4 %collective-permute-start.1 = (bf16[2,256,512]{1,2,0:T(8,128)(2,1)S(1)}, bf16[2,256,512]{1,2,0:T(8,128)(2,1)}, u32[]{:S(2)}, u32[]{:S(2)}) collective-permute-start(bf16[2,256,512]{1,2,0:T(8,128)(2,1)S(1)} %pad_maximum_fusion.2), channel_id=1, source_target_pairs={{2,0},{4,2},{6,4},{8,6},{10,8},{12,10},{14,12},{16,14},{18,16},{20... | collective-permute-start | bytes 1572872 | tf_op jit(solution)/shard_map/ppermute | solution.py:21
  16.6 12.5 %copy-start.5 = (bf16[256,512]{1,0:T(8,128)(2,1)S(1)}, bf16[256,512]{1,0:T(8,128)(2,1)}, u32[]{:S(2)}) copy-start(bf16[256,512]{1,0:T(8,128)(2,1)} %param.12) | copy-start | bytes 786436
  31.8 1.9 copy-start.6
  31.8 32.8 %copy-start.3 = (bf16[128,2048]{1,0:T(8,128)(2,1)S(1)}, bf16[128,2048]{1,0:T(8,128)(2,1)}, u32[]{:S(2)}) copy-start(bf16[128,2048]{1,0:T(8,128)(2,1)} %param.15) | copy-start | bytes 1572868
  31.8 34.1 %copy-start.7 = (f32[2048]{0:T(1024)S(1)}, f32[2048]{0:T(1024)}, u32[]{:S(2)}) copy-start(f32[2048]{0:T(1024)} %param.18) | copy-start | bytes 24580
  33.6 209.3 %reduce-scatter.2.cloned.1.call-start = ((), (), s32[]{:S(2)}) async-start(), calls=%async_computation.5 | async-start | bytes 18874368 | tf_op jit(solution)/shard_map/reduce_scatter | solution.py:107
  176.4 18.5 %copy-start.9 = (bf16[1,2048,352]{1,2,0:T(8,128)(2,1)S(1)}, bf16[1,2048,352]{1,2,0:T(8,128)(2,1)}, u32[]{:S(2)}) copy-start(bf16[1,2048,352]{1,2,0:T(8,128)(2,1)} %param.21) | copy-start | bytes 4325380
  190.4 4.5 %copy-start.2 = (bf16[2,1536,2048]{2,1,0:T(8,128)(2,1)}, bf16[2,1536,2048]{2,1,0:T(8,128)(2,1)S(1)}, u32[]{:S(2)}) copy-start(bf16[2,1536,2048]{2,1,0:T(8,128)(2,1)S(1)} %all_to_all.16) | copy-start | bytes 37748740
  242.8 10.7 %copy-start.8 = (f32[128,6]{0,1:T(8,128)S(1)}, f32[128,6]{0,1:T(8,128)}, u32[]{:S(2)}) copy-start(f32[128,6]{0,1:T(8,128)} %param.20) | copy-start | bytes 9220
  242.8 97.7 %all-to-all-start.2 = ((bf16[64,24,2048]{2,1,0:T(8,128)(2,1)}), bf16[64,24,2048]{2,1,0:T(8,128)(2,1)}, u32[]{:S(2)}, u32[]{:S(2)}) async-start(bf16[64,24,2048]{2,1,0:T(8,128)(2,1)} %bitcast.77), calls=%async_computation.3 | async-start | bytes 12582912 | tf_op jit(solution)/shard_map/all_to_all | solution.py:29
  351.3 11.2 %copy-start.1 = (bf16[512,2048]{1,0:T(8,128)(2,1)S(1)}, bf16[512,2048]{1,0:T(8,128)(2,1)}, u32[]{:S(2)}) copy-start(bf16[512,2048]{1,0:T(8,128)(2,1)} %param.17) | copy-start | bytes 6291460
  357.7 3.5 copy-start.4
Sparse Core Ops, SparseCore 0:
  33.7 30.8 all-reduce.2
  220.0 22.8 reduce-scatter.1
